TPU v7x, 512 devices: a whole 4x8x8 slice. The times are simulated.
512 devices in a mesh: wide: 64 (over y, z_lo, x), narrow: 8 (over z_hi, core).
Axes of the slice: x: 4, y: 8, z: 8 (z_hi: 4, z_lo: 2; z = z_hi * 2 + z_lo), core: 2. Of those that a mesh axis runs over, the one named last changes fastest.
Arguments:
- conc: float32 [2, 128, 64, 1024], P(None, 'wide', 'narrow'), may hold values from 0.2 to 2
- potential: float32 [128, 64, 1024], P('wide', 'narrow'), may hold values from -6 to 6
- velocity: float32 [3, 128, 64, 1024], P(None, 'wide', 'narrow'), may hold values from -3 to 3
- solid: int32 [128, 64, 1024], P('wide', 'narrow'), may hold values 0 or 1
- fixed_charge: float32 [128, 64, 1024], P('wide', 'narrow'), may hold values from -6 to 6
Outputs:
- new_conc: float32 [2, 128, 64, 1024], P(None, 'wide', 'narrow')
- new_potential: float32 [128, 64, 1024], P('wide', 'narrow')
All inputs are finite; a program needn't handle non-finite values. No bound on the sum of `solid` on one device may be relied on, other than what follows from the above.
Results may differ from a plain program's by a relative error of at most 0.0001.
Values sent between devices are 32-bit elements; how exact they have to be, the bound alone decides.
A program may use at most 64 MiB of HBM per device.

v0:
```python
import jax
import jax.numpy as jnp
from jax import lax
from jax.sharding import PartitionSpec as P

band_fills = (0.0, 1.0, 0.0, 0.0)


def with_halo(cells, sides, width):
    for axis, dim in sides:
        count = lax.axis_size(axis)
        ends = count - 1
        head = lax.slice_in_dim(cells, 0, width, axis=dim)
        tail = lax.slice_in_dim(cells, cells.shape[dim] - width, cells.shape[dim], axis=dim)
        cells = jnp.concatenate(
            [
                lax.ppermute(tail, axis, [(i, (i + 1) % count) for i in range(ends)]),
                cells,
                lax.ppermute(head, axis, [((i + 1) % count, i) for i in range(ends)]),
            ],
            axis=dim,
        )
    return cells


def inner_part(array, axis, margin):
    return lax.slice_in_dim(array, margin, array.shape[axis] - margin, axis=axis)


def explicit_rhs(padded, fixed_charge):
    mobility = jnp.array([0.25, -0.25], jnp.float32).reshape(2, 1, 1, 1)
    total = None
    for direction in (1, 2, 3):
        sub = padded
        for other in (1, 2, 3):
            if other != direction:
                sub = inner_part(sub, other, 2)
        field = sub[2]
        length = field.shape[direction - 1]
        grad = (
            lax.slice_in_dim(field, 2, length, axis=direction - 1)
            - lax.slice_in_dim(field, 0, length - 2, axis=direction - 1)
        ) * 0.5
        inner = inner_part(sub, direction, 1)
        flux = inner[6][None] * inner[0:2] * (inner[2 + direction][None] - mobility * grad[None])
        size = flux.shape[direction]
        diverge = (
            lax.slice_in_dim(flux, 2, size, axis=direction)
            - lax.slice_in_dim(flux, 0, size - 2, axis=direction)
        ) * 0.5
        total = diverge if total is None else total + diverge
    core = padded
    for axis in (1, 2, 3):
        core = inner_part(core, axis, 2)
    fluid = core[6]
    rhs_conc = fluid[None] * (core[0:2] - 0.5 * total)
    charge = fluid * (core[0] - core[1]) + (1.0 - fluid) * fixed_charge
    rhs_field = core[2] + 2.0 * charge
    return jnp.concatenate([rhs_conc, rhs_field[None], fluid[None]], 0)


def shifted(array, dim, spacing, fill_value):
    length = array.shape[dim]
    pad_shape = list(array.shape)
    pad_shape[dim] = abs(spacing)
    filler = jnp.full(tuple(pad_shape), fill_value, array.dtype)
    if spacing > 0:
        return jnp.concatenate(
            [filler, lax.slice_in_dim(array, 0, length - spacing, axis=dim)], dim
        )
    return jnp.concatenate([lax.slice_in_dim(array, -spacing, length, axis=dim), filler], dim)


def make_coeffs(fluid, mask_prev, mask_next, inside_prev, inside_next):
    lower_band = jnp.stack(
        [-8.0 * fluid * mask_prev, -5.0 * fluid * mask_prev, -16.0 * inside_prev]
    )
    upper_band = jnp.stack(
        [-8.0 * fluid * mask_next, -5.0 * fluid * mask_next, -16.0 * inside_next]
    )
    both_sides = mask_prev + mask_next
    main_band = jnp.stack(
        [1.0 + 8.0 * fluid * both_sides, 1.0 + 5.0 * fluid * both_sides, jnp.full_like(fluid, 33.0)]
    )
    return (lower_band, main_band, upper_band)


def local_coeffs(block, dim):
    fluid = block[3]
    fluid_dim = dim - 1
    ones_field = jnp.ones_like(fluid)
    return make_coeffs(
        fluid,
        shifted(fluid, fluid_dim, 1, 0.0),
        shifted(fluid, fluid_dim, -1, 0.0),
        shifted(ones_field, fluid_dim, 1, 0.0),
        shifted(ones_field, fluid_dim, -1, 0.0),
    )


def local_neighbours(dim):

    def neighbours(bands, spacing):
        before = tuple(
            (
                shifted(value, dim, spacing, fill_value)
                for value, fill_value in zip(bands, band_fills)
            )
        )
        after = tuple(
            (
                shifted(value, dim, -spacing, fill_value)
                for value, fill_value in zip(bands, band_fills)
            )
        )
        return (before, after)

    return neighbours


def cyclic_solve(lower_band, main_band, upper_band, source, length, neighbours):
    spacing = 1
    while spacing < length:
        before, after = neighbours((lower_band, main_band, upper_band, source), spacing)
        factor_prev = -lower_band / before[1]
        factor_next = -upper_band / after[1]
        new_lower = factor_prev * before[0]
        new_upper = factor_next * after[2]
        main_band = main_band + factor_prev * before[2] + factor_next * after[0]
        source = source + factor_prev * before[3] + factor_next * after[3]
        lower_band, upper_band = (new_lower, new_upper)
        spacing = spacing * 2
    return source / main_band


def solve_block(block, dim):
    lower_band, main_band, upper_band = local_coeffs(block, dim)
    return cyclic_solve(
        lower_band, main_band, upper_band, block[:3], block.shape[dim], local_neighbours(dim)
    )


def solve_along_y(block):
    return solve_block(block, 2)


def shards(conc, potential, velocity, solid, fixed_charge):
    fluid = (1 - solid).astype(jnp.float32)
    stacked = jnp.concatenate([conc, potential[None], velocity, fluid[None]], 0)
    padded = with_halo(stacked, (("wide", 1), ("narrow", 2)), 2)
    padded = jnp.pad(padded, ((0, 0), (0, 0), (0, 0), (2, 2)))
    rhs = explicit_rhs(padded, fixed_charge)
    width = rhs.shape[1]
    depth = rhs.shape[2]
    height = rhs.shape[3]
    flat = rhs.reshape(4, width, depth * height)
    lines = lax.all_to_all(flat, "wide", split_axis=2, concat_axis=1, tiled=True)
    solved = solve_block(lines, 1)
    returned = lax.all_to_all(solved, "wide", split_axis=1, concat_axis=2, tiled=True).reshape(
        3, width, depth, height
    )
    tiles = jnp.concatenate([returned, fluid[None]], 0)
    y_solved = solve_along_y(
        lax.all_to_all(tiles, "narrow", split_axis=3, concat_axis=2, tiled=True)
    )
    after_y = lax.all_to_all(y_solved, "narrow", split_axis=2, concat_axis=3, tiled=True)
    result = solve_block(jnp.concatenate([after_y, fluid[None]], 0), 3)
    return (result[:2], result[2])


def solution(mesh):
    return jax.shard_map(
        shards,
        mesh=mesh,
        in_specs=(
            P(None, "wide", "narrow", None),
            P("wide", "narrow", None),
            P(None, "wide", "narrow", None),
            P("wide", "narrow", None),
            P("wide", "narrow", None),
        ),
        out_specs=(P(None, "wide", "narrow", None), P("wide", "narrow", None)),
        check_vma=False,
    )
```

profile of v0, /device:TPU:1, one launch (start us, length us, event | category | flops | bytes accessed | tf_op | source)
XLA Modules:
  0.0 214.5 jit_solution(8017876829515559526)
XLA Ops:
  2.6 4.0 %collective-permute-start = (f32[7,2,8,1024]{3,2,1,0:T(8,128)S(1)}, f32[7,2,8,1024]{3,2,1,0:T(8,128)S(1)}, u32[]{:S(2)}, u32[]{:S(2)}) collective-permute-start(f32[7,2,8,1024]{3,2,1,0:T(8,128)S(1)} %pad_maximum_fusion.1), channel_id=1, source_target_pairs={{0,8},{8,16},{16,24},{24,32},{32,40},{40,48},{48,56},{56,64},{64,7... | collective-permute-start | bytes 1376264 | tf_op jit(solution)/shard_map/ppermute | solution.py:17
  6.6 1.3 collective-permute-start.1
  9.2 3.2 %collective-permute-done = f32[7,2,8,1024]{3,2,1,0:T(8,128)S(1)} collective-permute-done((f32[7,2,8,1024]{3,2,1,0:T(8,128)S(1)}, f32[7,2,8,1024]{3,2,1,0:T(8,128)S(1)}, u32[]{:S(2)}, u32[]{:S(2)}) %collective-permute-start) | collective-permute-done | bytes 458784 | tf_op jit(solution)/shard_map/ppermute | solution.py:17
  12.4 3.9 %collective-permute-done.1 = f32[7,2,8,1024]{3,2,1,0:T(8,128)S(1)} collective-permute-done((f32[7,2,8,1024]{3,2,1,0:T(8,128)S(1)}, f32[7,2,8,1024]{3,2,1,0:T(8,128)S(1)}, u32[]{:S(2)}, u32[]{:S(2)}) %collective-permute-start.1) | collective-permute-done | bytes 458784 | tf_op jit(solution)/shard_map/ppermute | solution.py:19
  16.3 1.5 pad_maximum_fusion.7
  18.0 10.8 %collective-permute-start.2 = (f32[7,6,2,1024]{3,0,2,1:T(8,128)S(1)}, f32[7,6,2,1024]{3,0,2,1:T(8,128)S(1)}, u32[]{:S(2)}, u32[]{:S(2)}) collective-permute-start(f32[7,6,2,1024]{3,0,2,1:T(8,128)S(1)} %copy.76), channel_id=1, source_target_pairs={{0,1},{1,2},{2,3},{3,4},{4,5},{5,6},{6,7},{8,9},{9,10},{10,11},{11... | collective-permute-start | bytes 1032200 | tf_op jit(solution)/shard_map/ppermute | solution.py:17
  29.1 1.9 collective-permute-start.3
  31.2 2.4 %collective-permute-done.2 = f32[7,6,2,1024]{3,0,2,1:T(8,128)S(1)} collective-permute-done((f32[7,6,2,1024]{3,0,2,1:T(8,128)S(1)}, f32[7,6,2,1024]{3,0,2,1:T(8,128)S(1)}, u32[]{:S(2)}, u32[]{:S(2)}) %collective-permute-start.2) | collective-permute-done | bytes 344096 | tf_op jit(solution)/shard_map/ppermute | solution.py:17
  33.9 9.4 %collective-permute-done.3 = f32[7,6,2,1024]{3,0,2,1:T(8,128)S(1)} collective-permute-done((f32[7,6,2,1024]{3,0,2,1:T(8,128)S(1)}, f32[7,6,2,1024]{3,0,2,1:T(8,128)S(1)}, u32[]{:S(2)}, u32[]{:S(2)}) %collective-permute-start.3) | collective-permute-done | bytes 344096 | tf_op jit(solution)/shard_map/ppermute | solution.py:19
  45.2 7.9 %copy.86 = f32[4,2,8192]{0,1,2:T(2,128)} copy(f32[4,2,8192]{2,1,0:T(2,128)S(1)} %pad_maximum_fusion.8) | data formatting | bytes 524288 | tf_op jit(solution)/shard_map/concatenate | solution.py:59
  53.0 14.9 %reshape.34 = f32[64,1,1024]{2,1,0:T(1,128)} reshape(f32[8192,2,4]{2,1,0:T(2,128)} %bitcast.115) | data formatting | bytes 524288
  67.9 14.3 %all-to-all-start = ((f32[64,1,1024]{2,1,0:T(1,128)}), f32[64,1,1024]{2,1,0:T(1,128)S(1)}, u32[]{:S(2)}, u32[]{:S(2)}) async-start(f32[64,1,1024]{2,1,0:T(1,128)} %reshape.34), calls=%async_computation | async-start | bytes 524288 | tf_op jit(solution)/shard_map/all_to_all | solution.py:157
  82.3 10.4 %all-to-all-done = f32[64,1,1024]{2,1,0:T(1,128)S(1)} async-done(((f32[64,1,1024]{2,1,0:T(1,128)}), f32[64,1,1024]{2,1,0:T(1,128)S(1)}, u32[]{:S(2)}, u32[]{:S(2)}) %all-to-all-start) | async-done | bytes 262176 | tf_op jit(solution)/shard_map/all_to_all | solution.py:157
  94.5 14.4 %reshape.35 = f32[8192,2,4]{2,1,0:T(2,128)} reshape(f32[64,1024]{1,0:T(8,128)S(1)} %reduce) | data formatting | bytes 524288
  108.9 9.4 %copy.87 = f32[4,2,64,128]{3,1,2,0:T(2,128)S(1)} copy(f32[4,2,64,128]{0,1,3,2:T(2,128)} %bitcast.116) | data formatting | bytes 524288 | tf_op jit(solution)/shard_map/all_to_all | solution.py:157
  121.9 14.9 %all_to_all.63 = f32[3,128,128]{2,0,1:T(4,128)S(1)} all-to-all(f32[3,128,128]{2,0,1:T(4,128)S(1)} %copy.88), channel_id=1, replica_groups=mesh['wide'=64,'narrow'=8] {'wide'}, dimensions={1} | all-to-all | bytes 393216 | tf_op jit(solution)/shard_map/all_to_all | solution.py:159
  136.9 4.3 %copy.90 = f32[4,2,8,1024]{2,1,0,3:T(2,128)} copy(f32[4,2,8,1024]{3,2,1,0:T(8,128)S(1)} %pad_maximum_fusion.9) | data formatting | bytes 524288 | tf_op jit(solution)/shard_map/concatenate | solution.py:162
  141.2 8.3 %reshape.36 = f32[8,1,8192]{2,1,0:T(1,128)S(1)} reshape(f32[1024,4,2,8]{3,2,1,0:T(2,128)} %bitcast.117) | data formatting | bytes 524288
  149.5 22.3 %all_to_all.64 = f32[8,1,8192]{2,1,0:T(1,128)S(1)} all-to-all(f32[8,1,8192]{2,1,0:T(1,128)S(1)} %reshape.36), channel_id=1, replica_groups=mesh['wide'=64,'narrow'=8] {'narrow'}, dimensions={0} | all-to-all | bytes 524288 | tf_op jit(solution)/shard_map/all_to_all | solution.py:164
  171.8 1.3 reduce.1
  173.1 8.4 %reshape.37 = f32[1024,4,2,8]{3,2,1,0:T(2,128)} reshape(f32[8,8192]{1,0:T(8,128)S(1)} %reduce.1) | data formatting | bytes 524288
  181.4 5.1 %copy.91 = f32[4,2,8,8,128]{4,2,3,1,0:T(8,128)S(1)} copy(f32[4,2,8,8,128]{2,1,0,4,3:T(2,128)} %bitcast.118) | data formatting | bytes 524288 | tf_op jit(solution)/shard_map/all_to_all | solution.py:164
  190.6 5.8 %all-to-all-start.3 = ((f32[3,2,64,128]{3,1,0,2:T(2,128)}), f32[3,2,64,128]{3,1,0,2:T(2,128)S(1)}, u32[]{:S(2)}, u32[]{:S(2)}) async-start(f32[3,2,64,128]{3,1,0,2:T(2,128)} %copy.92), calls=%async_computation.3 | async-start | bytes 393216 | tf_op jit(solution)/shard_map/all_to_all | solution.py:166
  196.6 9.2 %all-to-all-done.3 = f32[3,2,64,128]{3,1,0,2:T(2,128)S(1)} async-done(((f32[3,2,64,128]{3,1,0,2:T(2,128)}), f32[3,2,64,128]{3,1,0,2:T(2,128)S(1)}, u32[]{:S(2)}, u32[]{:S(2)}) %all-to-all-start.3) | async-done | bytes 196640 | tf_op jit(solution)/shard_map/all_to_all | solution.py:166
  (203 shorter events, 23.4 us)
Async XLA Ops:
  1.5 29.5 %copy-start = (f32[2,2,8,1024]{3,2,1,0:T(8,128)S(1)}, f32[2,2,8,1024]{3,2,1,0:T(8,128)}, u32[]{:S(2)}) copy-start(f32[2,2,8,1024]{3,2,1,0:T(8,128)} %param.6) | copy-start | bytes 393220
  1.5 29.5 %copy-start.1 = (f32[3,2,8,1024]{3,2,1,0:T(8,128)S(1)}, f32[3,2,8,1024]{3,2,1,0:T(8,128)}, u32[]{:S(2)}) copy-start(f32[3,2,8,1024]{3,2,1,0:T(8,128)} %param.8) | copy-start | bytes 589828
  1.5 29.5 %copy-start.2 = (f32[2,8,1024]{2,1,0:T(8,128)S(1)}, f32[2,8,1024]{2,1,0:T(8,128)}, u32[]{:S(2)}) copy-start(f32[2,8,1024]{2,1,0:T(8,128)} %param.7) | copy-start | bytes 196612
  2.6 9.8 %collective-permute-start = (f32[7,2,8,1024]{3,2,1,0:T(8,128)S(1)}, f32[7,2,8,1024]{3,2,1,0:T(8,128)S(1)}, u32[]{:S(2)}, u32[]{:S(2)}) collective-permute-start(f32[7,2,8,1024]{3,2,1,0:T(8,128)S(1)} %pad_maximum_fusion.1), channel_id=1, source_target_pairs={{0,8},{8,16},{16,24},{24,32},{32,40},{40,48},{48,56},{56,64},{64,7... | collective-permute-start | bytes 1376264 | tf_op jit(solution)/shard_map/ppermute | solution.py:17
  6.6 9.7 %collective-permute-start.1 = (f32[7,2,8,1024]{3,2,1,0:T(8,128)S(1)}, f32[7,2,8,1024]{3,2,1,0:T(8,128)S(1)}, u32[]{:S(2)}, u32[]{:S(2)}) collective-permute-start(f32[7,2,8,1024]{3,2,1,0:T(8,128)S(1)} %pad_maximum_fusion.1), channel_id=1, source_target_pairs={{8,0},{16,8},{24,16},{32,24},{40,32},{48,40},{56,48},{64,56},{72,6... | collective-permute-start | bytes 1376264 | tf_op jit(solution)/shard_map/ppermute | solution.py:19
  17.8 13.3 %copy-start.9 = (f32[2]{0:T(128)S(1)}, f32[2]{0:T(128)}, u32[]{:S(2)}) copy-start(f32[2]{0:T(128)} %constant.35.clone) | copy-start | bytes 28
  18.0 15.6 %collective-permute-start.2 = (f32[7,6,2,1024]{3,0,2,1:T(8,128)S(1)}, f32[7,6,2,1024]{3,0,2,1:T(8,128)S(1)}, u32[]{:S(2)}, u32[]{:S(2)}) collective-permute-start(f32[7,6,2,1024]{3,0,2,1:T(8,128)S(1)} %copy.76), channel_id=1, source_target_pairs={{0,1},{1,2},{2,3},{3,4},{4,5},{5,6},{6,7},{8,9},{9,10},{10,11},{11... | collective-permute-start | bytes 1032200 | tf_op jit(solution)/shard_map/ppermute | solution.py:17
  29.1 14.2 %collective-permute-start.3 = (f32[7,6,2,1024]{3,0,2,1:T(8,128)S(1)}, f32[7,6,2,1024]{3,0,2,1:T(8,128)S(1)}, u32[]{:S(2)}, u32[]{:S(2)}) collective-permute-start(f32[7,6,2,1024]{3,0,2,1:T(8,128)S(1)} %copy.77), channel_id=1, source_target_pairs={{1,0},{2,1},{3,2},{4,3},{5,4},{6,5},{7,6},{9,8},{10,9},{11,10},{12... | collective-permute-start | bytes 1032200 | tf_op jit(solution)/shard_map/ppermute | solution.py:19
  67.9 24.8 %all-to-all-start = ((f32[64,1,1024]{2,1,0:T(1,128)}), f32[64,1,1024]{2,1,0:T(1,128)S(1)}, u32[]{:S(2)}, u32[]{:S(2)}) async-start(f32[64,1,1024]{2,1,0:T(1,128)} %reshape.34), calls=%async_computation | async-start | bytes 524288 | tf_op jit(solution)/shard_map/all_to_all | solution.py:157
  118.3 0.8 copy-start.7
  118.3 0.9 copy-start.8
  186.6 0.9 copy-start.5
  186.6 0.9 copy-start.6
  189.6 16.3 %copy-start.3 = (f32[1,2,8,1024]{3,2,1,0:T(8,128)S(1)}, f32[1,2,8,1024]{3,2,1,0:T(8,128)}, u32[]{:S(2)}) copy-start(f32[1,2,8,1024]{3,2,1,0:T(8,128)} %constant.33.clone.1) | copy-start | bytes 196612
  189.6 16.3 %copy-start.4 = (f32[1,2,8,1024]{3,2,1,0:T(8,128)S(1)}, f32[1,2,8,1024]{3,2,1,0:T(8,128)}, u32[]{:S(2)}) copy-start(f32[1,2,8,1024]{3,2,1,0:T(8,128)} %constant.34.clone.1) | copy-start | bytes 196612
  190.6 15.1 %all-to-all-start.3 = ((f32[3,2,64,128]{3,1,0,2:T(2,128)}), f32[3,2,64,128]{3,1,0,2:T(2,128)S(1)}, u32[]{:S(2)}, u32[]{:S(2)}) async-start(f32[3,2,64,128]{3,1,0,2:T(2,128)} %copy.92), calls=%async_computation.3 | async-start | bytes 393216 | tf_op jit(solution)/shard_map/all_to_all | solution.py:166
where the time goes:
time: 215 us
  local copies, waits for them, and re-layouts  83 us (39%)
  waiting for transfers between devices  38.5 us (18%)
  starting transfers between devices  38.1 us (18%)
  blocking collectives  37.2 us (17%)
  other arithmetic  15.6 us (7%)
    unnamed x24, local copies, waits for them, and re-layouts  47.2 us
    all_to_all x1, blocking collectives, shards(): lax.all_to_all(tiles, 'narrow', split_axis=3, concat_axis=2, tiled=True)  22.3 us
    all_to_all x1, blocking collectives, shards(): lax.all_to_all(solved, 'wide', split_axis=1, concat_axis=2, tiled=True)  14.9 us
    ppermute x2, starting transfers between devices, with_halo(): lax.ppermute(tail, axis, [(i, (i + 1) % count) for i in range(ends)])  14.8 us
    all_to_all x1, starting transfers between devices, shards(): lax.all_to_all(flat, 'wide', split_axis=2, concat_axis=1, tiled=True)  14.3 us
    ppermute x2, waiting for transfers between devices, with_halo(): lax.ppermute(head, axis, [((i + 1) % count, i) for i in range(ends)])  13.3 us
    all_to_all x1, waiting for transfers between devices, shards(): lax.all_to_all(flat, 'wide', split_axis=2, concat_axis=1, tiled=True)  10.4 us
    all_to_all x2, local copies, waits for them, and re-layouts, shards(): lax.all_to_all(flat, 'wide', split_axis=2, concat_axis=1, tiled=True)  9.93 us
  transfers between devices with their start and end apart: 6, of which 6 were waited for; matrix products, arithmetic and copies ran while one was open for 1% of the time, Pallas kernels for 0%

commit v1 on v0

v1 whole, which is shorter than its diff:
```python
import jax
import jax.numpy as jnp
from jax import lax
from jax.experimental import pallas as pl
from jax.experimental.pallas import tpu as pltpu
from jax.sharding import PartitionSpec as P

F32 = jnp.float32
MESH = pl.DeviceIdType.MESH
LANES = 128
ROWS = 8
CHUNK = 8


def pcr(here, prev, succ):
    a, c, d = here
    ap, cp, dp = prev
    an, cn, dn = succ
    r = 1.0 / (1.0 - a * cp - c * an)
    return -(a * ap) * r, -(c * cn) * r, (d - a * dp - c * dn) * r


def row_facts():
    row = lax.broadcasted_iota(jnp.int32, (1, ROWS, LANES), 1)
    even = row % 2 == 0
    is_pot = row >= 4
    rate = jnp.where(row < 2, 8.0, jnp.where(row < 4, 5.0, jnp.where(row < 6, 16.0, 0.0)))
    return even, is_pot, rate.astype(F32)


def masks(tiles):
    return tiles[:, 6:7, :], tiles[:, 7:8, :]


def normal_bands(tiles, mask, mask_prev, mask_next, rate, is_first, is_last):
    rm = rate * mask
    inv = 1.0 / (1.0 + rm * (mask_prev + mask_next))
    lower = jnp.where(is_first, 0.0, -rm * mask_prev * inv)
    upper = jnp.where(is_last, 0.0, -rm * mask_next * inv)
    return lower, upper, tiles * inv


def solve_tiles(src_ref, src_pad, bufs, dst_ref, dst_pad, count, pad, paired):
    def build(i, _):
        even, is_pot, rate = row_facts()
        base = src_pad + i * CHUNK
        tiles = src_ref[pl.ds(base, CHUNK)]
        m0, m1 = masks(tiles)
        p0, p1 = masks(src_ref[pl.ds(base - 1, CHUNK)])
        n0, n1 = masks(src_ref[pl.ds(base + 1, CHUNK)])
        own = jnp.where(is_pot, 1.0, jnp.where(even, m0, m1))
        place = i * CHUNK + lax.broadcasted_iota(jnp.int32, (CHUNK, ROWS, LANES), 0)
        first = place == 0
        last = place == count - 1
        if paired:
            before = jnp.where(is_pot, 1.0, jnp.where(even, p1, m0))
            after = jnp.where(is_pot, 1.0, jnp.where(even, m1, n0))
            first = first & even
            last = last & jnp.logical_not(even)
        else:
            before = jnp.where(is_pot, 1.0, jnp.where(even, p0, p1))
            after = jnp.where(is_pot, 1.0, jnp.where(even, n0, n1))
        bands = normal_bands(tiles, own, before, after, rate, first, last)
        for k in range(3):
            bufs[0][k, pl.ds(pad + i * CHUNK, CHUNK)] = bands[k]
        return 0

    lax.fori_loop(0, count // CHUNK, build, 0)
    now = 0

    def window(buf, base):
        return tuple(buf[k, pl.ds(base, CHUNK)] for k in range(3))

    if paired:

        def pair_step(i, _):
            even, _, _ = row_facts()
            base = pad + i * CHUNK
            here = window(bufs[0], base)
            left = window(bufs[0], base - 1)
            right = window(bufs[0], base + 1)

            def up(v):
                return pltpu.roll(v, ROWS - 1, 1)

            def down(v):
                return pltpu.roll(v, 1, 1)

            prev = tuple(jnp.where(even, up(l), down(h)) for l, h in zip(left, here))
            succ = tuple(jnp.where(even, up(h), down(r)) for h, r in zip(here, right))
            for k, v in enumerate(pcr(here, prev, succ)):
                bufs[1][k, pl.ds(base, CHUNK)] = v
            return 0

        lax.fori_loop(0, count // CHUNK, pair_step, 0)
        now = 1

    spacing = 1
    while spacing < count:
        source, target = bufs[now], bufs[1 - now]
        final = spacing * 2 >= count

        def step(i, _, source=source, target=target, spacing=spacing, final=final):
            base = pad + i * CHUNK
            new = pcr(
                window(source, base), window(source, base - spacing), window(source, base + spacing)
            )
            if final:
                dst_ref[pl.ds(dst_pad + i * CHUNK, CHUNK)] = new[2]
            else:
                for k in range(3):
                    target[k, pl.ds(base, CHUNK)] = new[k]
            return 0

        lax.fori_loop(0, count // CHUNK, step, 0)
        now = 1 - now
        spacing *= 2


def main_kernel(
    nw, nn, conc, pot, vel, solid, fixed, out,
    sx_r, sx_l, rx_l, rx_r, sy_u, sy_d, ry_d, ry_u, packed, stage, xr, xsol, xback,
    yr, ysol, buf_a, buf_b,
    hs, hr, xs_s, xs_r, xb_s, xb_r, ys_s, ys_r, yb_s, yb_r,
):
    wide = lax.axis_index("wide")
    narrow = lax.axis_index("narrow")
    right = lax.rem(wide + 1, nw)
    left = lax.rem(wide + nw - 1, nw)
    upper = lax.rem(narrow + 1, nn)
    lower = lax.rem(narrow + nn - 1, nn)
    zt = pot.shape[2] // LANES
    pad = (buf_a.shape[1] - nw) // 2

    barrier = pltpu.get_barrier_semaphore()

    def greet_wide(k, _):
        pl.semaphore_signal(
            barrier, inc=1, device_id={"wide": lax.rem(wide + k, nw)}, device_id_type=MESH
        )
        return 0

    def greet_narrow(k, _):
        pl.semaphore_signal(
            barrier, inc=1, device_id={"narrow": lax.rem(narrow + k, nn)}, device_id_type=MESH
        )
        return 0

    lax.fori_loop(1, nw, greet_wide, 0)
    lax.fori_loop(1, nn, greet_narrow, 0)

    fl = [(1 - solid[x]).astype(F32) for x in range(2)]
    act = [[fl[x] * conc[k, x] for x in range(2)] for k in range(2)]
    for k in range(2):
        sx_r[k] = act[k][1]
        sx_l[k] = act[k][0]
    sx_r[2] = vel[0, 1]
    sx_l[2] = vel[0, 0]
    for x in range(2):
        sx_r[3 + x] = pot[x]
        sx_l[3 + x] = pot[x]
        for k in range(2):
            sy_u[x, k : k + 1] = act[k][x][7:8]
            sy_d[x, k : k + 1] = act[k][x][0:1]
        sy_u[x, 2:3] = vel[1, x, 7:8]
        sy_d[x, 2:3] = vel[1, x, 0:1]
        sy_u[x, 3:5] = pot[x, 6:8]
        sy_d[x, 3:5] = pot[x, 0:2]
        sy_u[x, 5:8] = jnp.zeros((3, pot.shape[2]), F32)
        sy_d[x, 5:8] = jnp.zeros((3, pot.shape[2]), F32)
    nothing = jnp.zeros((pad, ROWS, LANES), F32)
    for buf in (buf_a, buf_b):
        for k in range(3):
            buf[k, pl.ds(0, pad)] = nothing
            buf[k, pl.ds(pad + nw, pad)] = nothing
    for ref in (xr, yr):
        ref[pl.ds(0, 1)] = nothing[:1]
        ref[pl.ds(nw + 1, 1)] = nothing[:1]

    pl.semaphore_wait(barrier, nw + nn - 2)

    halos = [
        pltpu.make_async_remote_copy(
            src_ref=src, dst_ref=dst, send_sem=hs.at[n], recv_sem=hr.at[n],
            device_id=peer, device_id_type=MESH,
        )
        for n, (src, dst, peer) in enumerate(
            (
                (sx_r, rx_l, {"wide": right}),
                (sx_l, rx_r, {"wide": left}),
                (sy_u, ry_d, {"narrow": upper}),
                (sy_d, ry_u, {"narrow": lower}),
            )
        )
    ]
    for copy in halos:
        copy.start()

    shape = (ROWS, pot.shape[2])
    lane = lax.broadcasted_iota(jnp.int32, shape, 1)
    sub = lax.broadcasted_iota(jnp.int32, shape, 0)
    length = pot.shape[2]

    def z_next(v):
        return jnp.where(lane == length - 1, 0.0, pltpu.roll(v, length - 1, 1))

    def z_prev(v):
        return jnp.where(lane == 0, 0.0, pltpu.roll(v, 1, 1))

    def y_next(v, edge):
        return jnp.where(sub == ROWS - 1, edge, pltpu.roll(v, ROWS - 1, 0))

    def y_prev(v, edge):
        return jnp.where(sub == 0, edge, pltpu.roll(v, 1, 0))

    tilt = (0.125, -0.125)
    div_z = []
    for x in range(2):
        p = pot[x]
        slope = z_next(p) - z_prev(p)
        row = []
        for k in range(2):
            q = act[k][x] * (vel[2, x] - tilt[k] * slope)
            row.append((z_next(q) - z_prev(q)) * 0.5)
        div_z.append(row)

    for copy in halos:
        copy.wait()

    has_left = wide > 0
    has_right = wide < nw - 1
    has_down = narrow > 0
    has_up = narrow < nn - 1

    def kept(flag, v):
        return jnp.where(flag, v, 0.0)

    def pack(row, v):
        for t in range(zt):
            packed[pl.ds((t * ROWS + row) * ROWS, ROWS), :] = v[:, t * LANES : (t + 1) * LANES]

    pots = [
        kept(has_left, rx_l[3]), kept(has_left, rx_l[4]), pot[0], pot[1],
        kept(has_right, rx_r[3]), kept(has_right, rx_r[4]),
    ]
    velx = [rx_l[2], vel[0, 0], vel[0, 1], rx_r[2]]
    for x in range(2):
        fixed_x = fixed[x]
        p = pot[x]
        down = kept(has_down, ry_d[x])
        up = kept(has_up, ry_u[x])
        slope_y = y_next(p, up[3:4]) - y_prev(p, down[4:5])
        slope_d = p[0:1] - down[3:4]
        slope_u = up[4:5] - p[7:8]
        for k in range(2):
            acts = [kept(has_left, rx_l[k]), act[k][0], act[k][1], kept(has_right, rx_r[k])]

            def flux_x(n):
                return acts[n] * (velx[n] - tilt[k] * (pots[n + 2] - pots[n]))

            div_x = (flux_x(x + 2) - flux_x(x)) * 0.5
            qy = act[k][x] * (vel[1, x] - tilt[k] * slope_y)
            q_down = down[k : k + 1] * (down[2:3] - tilt[k] * slope_d)
            q_up = up[k : k + 1] * (up[2:3] - tilt[k] * slope_u)
            div_y = (y_next(qy, q_up) - y_prev(qy, q_down)) * 0.5
            total = div_x + div_y + div_z[x][k]
            pack(2 * k + x, fl[x] * (conc[k, x] - 0.5 * total))
        charge = fl[x] * (conc[0, x] - conc[1, x]) + (1.0 - fl[x]) * fixed_x
        pack(4 + x, p + 2.0 * charge)
        pack(6 + x, fl[x])

    for t in range(zt):
        for y in range(ROWS):
            stage[t * ROWS + y] = packed[pl.ds(t * ROWS * ROWS + y, ROWS, stride=ROWS), :]

    def x_copy(k):
        peer = lax.rem(wide + k, nw)
        return pltpu.make_async_remote_copy(
            src_ref=stage.at[peer], dst_ref=xr.at[wide + 1],
            send_sem=xs_s.at[peer], recv_sem=xs_r.at[wide],
            device_id={"wide": peer}, device_id_type=MESH,
        )

    def x_arrival(k):
        peer = lax.rem(wide + k, nw)
        return pltpu.make_async_remote_copy(
            src_ref=stage.at[peer], dst_ref=xr.at[peer + 1],
            send_sem=xs_s.at[peer], recv_sem=xs_r.at[peer],
            device_id={"wide": peer}, device_id_type=MESH,
        )

    def back_copy(k):
        peer = lax.rem(wide + k, nw)
        return pltpu.make_async_remote_copy(
            src_ref=xsol.at[peer], dst_ref=xback.at[wide],
            send_sem=xb_s.at[peer], recv_sem=xb_r.at[wide],
            device_id={"wide": peer}, device_id_type=MESH,
        )

    def back_arrival(k):
        peer = lax.rem(wide + k, nw)
        return pltpu.make_async_remote_copy(
            src_ref=xsol.at[peer], dst_ref=xback.at[peer],
            send_sem=xb_s.at[peer], recv_sem=xb_r.at[peer],
            device_id={"wide": peer}, device_id_type=MESH,
        )

    def group(index):
        return pl.ds(pl.multiple_of(index * ROWS, ROWS), ROWS)

    def y_copy(k):
        peer = lax.rem(narrow + k, nn)
        return pltpu.make_async_remote_copy(
            src_ref=xback.at[group(peer)], dst_ref=yr.at[pl.ds(narrow * ROWS + 1, ROWS)],
            send_sem=ys_s.at[peer], recv_sem=ys_r.at[narrow],
            device_id={"narrow": peer}, device_id_type=MESH,
        )

    def y_arrival(k):
        peer = lax.rem(narrow + k, nn)
        return pltpu.make_async_remote_copy(
            src_ref=xback.at[group(peer)], dst_ref=yr.at[pl.ds(peer * ROWS + 1, ROWS)],
            send_sem=ys_s.at[peer], recv_sem=ys_r.at[peer],
            device_id={"narrow": peer}, device_id_type=MESH,
        )

    def out_copy(k):
        peer = lax.rem(narrow + k, nn)
        return pltpu.make_async_remote_copy(
            src_ref=ysol.at[group(peer)], dst_ref=out.at[group(narrow)],
            send_sem=yb_s.at[peer], recv_sem=yb_r.at[narrow],
            device_id={"narrow": peer}, device_id_type=MESH,
        )

    def out_arrival(k):
        peer = lax.rem(narrow + k, nn)
        return pltpu.make_async_remote_copy(
            src_ref=ysol.at[group(peer)], dst_ref=out.at[group(peer)],
            send_sem=yb_s.at[peer], recv_sem=yb_r.at[peer],
            device_id={"narrow": peer}, device_id_type=MESH,
        )

    def start(copy_of, count):
        def body(k, _):
            copy_of(k).start()
            return 0

        lax.fori_loop(1, count, body, 0)

    def arrive(copy_of, count):
        def body(k, _):
            copy_of(k).wait_recv()
            return 0

        lax.fori_loop(1, count, body, 0)

    def drain(copy_of, count):
        def body(k, _):
            copy_of(k).wait_send()
            return 0

        lax.fori_loop(1, count, body, 0)

    bufs = (buf_a, buf_b)
    start(x_copy, nw)
    xr[pl.ds(wide + 1, 1)] = stage[pl.ds(wide, 1)]
    arrive(x_arrival, nw)
    solve_tiles(xr, 1, bufs, xsol, 0, nw, pad, True)
    start(back_copy, nw)
    xback[pl.ds(wide, 1)] = xsol[pl.ds(wide, 1)]
    arrive(back_arrival, nw)
    start(y_copy, nn)
    yr[pl.ds(narrow * ROWS + 1, ROWS)] = xback[group(narrow)]
    arrive(y_arrival, nn)
    solve_tiles(yr, 1, bufs, ysol, 0, nn * ROWS, pad, False)
    start(out_copy, nn)
    out[group(narrow)] = ysol[group(narrow)]
    arrive(out_arrival, nn)
    drain(x_copy, nw)
    drain(back_copy, nw)
    drain(y_copy, nn)
    drain(out_copy, nn)


def z_kernel(tiles, solid, new_conc, new_pot):
    length = solid.shape[2]
    shape = (ROWS, length)
    lane = lax.broadcasted_iota(jnp.int32, shape, 1)
    first = lane == 0
    last = lane == length - 1

    def source(row):
        return jnp.concatenate(
            [
                tiles[pl.ds(t * ROWS * ROWS + row, ROWS, stride=ROWS), :]
                for t in range(length // LANES)
            ],
            axis=1,
        )

    def solve(lower, upper, sources):
        spacing = 1
        while spacing < length:
            lower_prev, upper_prev = (pltpu.roll(v, spacing, 1) for v in (lower, upper))
            lower_next, upper_next = (pltpu.roll(v, length - spacing, 1) for v in (lower, upper))
            r = 1.0 / (1.0 - lower * upper_prev - upper * lower_next)
            sources = [
                (d - lower * pltpu.roll(d, spacing, 1) - upper * pltpu.roll(d, length - spacing, 1)) * r
                for d in sources
            ]
            lower, upper = -(lower * lower_prev) * r, -(upper * upper_next) * r
            spacing *= 2
        return sources

    for x in range(2):
        mask = (1 - solid[x]).astype(F32)
        before = jnp.where(first, 0.0, pltpu.roll(mask, 1, 1))
        after = jnp.where(last, 0.0, pltpu.roll(mask, length - 1, 1))
        for k, rate in enumerate((8.0, 5.0)):
            rm = rate * mask
            inv = 1.0 / (1.0 + rm * (before + after))
            (result,) = solve(
                -rm * before * inv, -rm * after * inv, [source(2 * k + x) * inv]
            )
            new_conc[k, x] = result
    inv = 1.0 / 33.0
    results = solve(
        jnp.where(first, 0.0, -16.0 * inv) * jnp.ones(shape, F32),
        jnp.where(last, 0.0, -16.0 * inv) * jnp.ones(shape, F32),
        [source(4) / 33.0, source(5) / 33.0],
    )
    for x in range(2):
        new_pot[x] = results[x]


def solution(mesh):
    nw, nn = mesh.shape["wide"], mesh.shape["narrow"]

    def shards(conc, potential, velocity, solid, fixed_charge):
        height = potential.shape[2]
        vmem = pl.BlockSpec(memory_space=pltpu.VMEM)
        tiles = (nw, ROWS, LANES)
        padded = (nw + 2, ROWS, LANES)
        plane = (5, ROWS, height)
        edge = (2, ROWS, height)
        bands = (3, 2 * nw, ROWS, LANES)
        dma = pltpu.SemaphoreType.DMA

        def body(*refs):
            main_kernel(nw, nn, *refs)

        after_y = pl.pallas_call(
            body,
            name="halo_x_y",
            out_shape=jax.ShapeDtypeStruct(tiles, F32),
            in_specs=[vmem] * 5,
            out_specs=vmem,
            scratch_shapes=[pltpu.VMEM(plane, F32)] * 4
            + [pltpu.VMEM(edge, F32)] * 4
            + [pltpu.VMEM((nw * ROWS, LANES), F32)]
            + [pltpu.VMEM(s, F32) for s in (tiles, padded, tiles, tiles, padded, tiles, bands, bands)]
            + [dma((4,)), dma((4,)), dma((nw,)), dma((nw,)), dma((nw,)), dma((nw,))]
            + [dma((nn,)), dma((nn,)), dma((nn,)), dma((nn,))],
            compiler_params=pltpu.CompilerParams(collective_id=0, has_side_effects=True),
        )(conc, potential, velocity, solid, fixed_charge)
        return pl.pallas_call(
            z_kernel,
            name="solve_z",
            out_shape=(
                jax.ShapeDtypeStruct(conc.shape, F32),
                jax.ShapeDtypeStruct(potential.shape, F32),
            ),
            in_specs=[vmem] * 2,
            out_specs=(vmem, vmem),
        )(after_y.reshape(nw * ROWS, LANES), solid)

    return jax.shard_map(
        shards,
        mesh=mesh,
        in_specs=(
            P(None, "wide", "narrow", None),
            P("wide", "narrow", None),
            P(None, "wide", "narrow", None),
            P("wide", "narrow", None),
            P("wide", "narrow", None),
        ),
        out_specs=(P(None, "wide", "narrow", None), P("wide", "narrow", None)),
        check_vma=False,
    )
```

time: 215 us -> 73.3 us (0.34)
  local copies, waits for them, and re-layouts: 83 us -> 0 us
  Pallas kernels: 0 us -> 72.5 us
  waiting for transfers between devices: 38.5 us -> 0 us
  starting transfers between devices: 38.1 us -> 0 us
  blocking collectives: 37.2 us -> 0 us
  other arithmetic: 15.6 us -> 0 us
    pallas_call x0 -> x2, Pallas kernels: none -> 72.5 us  [the longest x1 67.8 us: shards(): pl.pallas_call(body, name='halo_x_y', out_shape=jax.ShapeDtypeStruct(tile...]
    unnamed x24 -> x0, local copies, waits for them, and re-layouts: 47.2 us -> none
    all_to_all x2 -> x0, blocking collectives: 37.2 us -> none  [the longest x1 22.3 us: shards(): lax.all_to_all(tiles, 'narrow', split_axis=3, concat_axis=2, tiled=True)]
    all_to_all x2 -> x0, starting transfers between devices: 20.1 us -> none  [the longest x1 14.3 us: shards(): lax.all_to_all(flat, 'wide', split_axis=2, concat_axis=1, tiled=True)]
    all_to_all x2 -> x0, waiting for transfers between devices: 19.5 us -> none  [the longest x1 10.4 us: shards(): lax.all_to_all(flat, 'wide', split_axis=2, concat_axis=1, tiled=True)]
    ppermute x4 -> x0, waiting for transfers between devices: 18.9 us -> none  [the longest x2 13.3 us: with_halo(): lax.ppermute(head, axis, [((i + 1) % count, i) for i in range(ends)])]
    ppermute x4 -> x0, starting transfers between devices: 18 us -> none  [the longest x2 14.8 us: with_halo(): lax.ppermute(tail, axis, [(i, (i + 1) % count) for i in range(ends)])]
    all_to_all x5 -> x0, local copies, waits for them, and re-layouts: 15.1 us -> none  [the longest x2 9.93 us: shards(): lax.all_to_all(flat, 'wide', split_axis=2, concat_axis=1, tiled=True)]
  transfers between devices with their start and end apart: 6 -> 0, of which waited for: 6 -> 0; matrix products, arithmetic and copies ran while one was open for 1% -> 0% of each run, Pallas kernels for 0% -> 0%
where the time goes in v1:
time: 73.3 us; the launch traced here: 73.2 us
  Pallas kernels  72.5 us (99%)
    pallas_call x1, Pallas kernels, shards(): pl.pallas_call(body, name='halo_x_y', out_shape=jax.ShapeDtypeStruct(tile...  67.8 us
    pallas_call x1, Pallas kernels, shards(): pl.pallas_call(z_kernel, name='solve_z', out_shape=(jax.ShapeDtypeStruct(...  4.75 us

profile of v1, /device:TPU:1, one launch (start us, length us, event | category | flops | bytes accessed | tf_op | source)
XLA Modules:
  0.0 73.2 jit_solution(17918765604927667708)
XLA Ops:
  0.6 67.8 %halo_x_y.1 = f32[64,8,128]{2,1,0:T(8,128)} custom-call(f32[2,2,8,1024]{3,2,1,0:T(8,128)} %refs_0_.1, f32[2,8,1024]{2,1,0:T(8,128)} %refs_1_.1, f32[3,2,8,1024]{3,2,1,0:T(8,128)} %refs_2_.1, s32[2,8,1024]{2,1,0:T(8,128)} %solid.1, f32[2,8,1024]{2,1,0:T(8,128)} %refs_4_.1), custom_call_target="tpu_custom_call" | custom-call | tf_op jit(solution)/shard_map/halo_x_y/pallas_call | solution.py:452
  68.4 4.7 %solve_z.1 = (f32[2,2,8,1024]{3,2,1,0:T(8,128)}, f32[2,8,1024]{2,1,0:T(8,128)}) custom-call(f32[512,128]{1,0:T(8,128)} %bitcast.1, s32[2,8,1024]{2,1,0:T(8,128)} %solid.1), custom_call_target="tpu_custom_call" | custom-call | tf_op jit(solution)/shard_map/solve_z/pallas_call | solution.py:466

commit v2 on v1

--- a/solution.py
+++ b/solution.py
@@ -120,8 +120,9 @@
 def main_kernel(
     nw, nn, conc, pot, vel, solid, fixed, out,
     sx_r, sx_l, rx_l, rx_r, sy_u, sy_d, ry_d, ry_u, packed, stage, xr, xsol, xback,
-    yr, ysol, buf_a, buf_b,
-    hs, hr, xs_s, xs_r, xb_s, xb_r, ys_s, ys_r, yb_s, yb_r,
+    buf_a, buf_b, y_am, y_m, y_c, y_left, y_right, y_sol,
+    edge_s, edge_r, dat_s, dat_r, ends_s, ends_r, ring,
+    hs, hr, xe_s, xe_r, xs_s, xs_r, xb_s, xb_r, yc_s, yc_r, ys_s, ys_r, yb_s, yb_r,
 ):
     wide = lax.axis_index("wide")
     narrow = lax.axis_index("narrow")
@@ -166,16 +167,80 @@
         sy_d[x, 2:3] = vel[1, x, 0:1]
         sy_u[x, 3:5] = pot[x, 6:8]
         sy_d[x, 3:5] = pot[x, 0:2]
-        sy_u[x, 5:8] = jnp.zeros((3, pot.shape[2]), F32)
-        sy_d[x, 5:8] = jnp.zeros((3, pot.shape[2]), F32)
+        sy_u[x, 5:6] = fl[x][7:8]
+        sy_d[x, 5:6] = fl[x][0:1]
+        sy_u[x, 6:8] = jnp.zeros((2, pot.shape[2]), F32)
+        sy_d[x, 6:8] = jnp.zeros((2, pot.shape[2]), F32)
     nothing = jnp.zeros((pad, ROWS, LANES), F32)
     for buf in (buf_a, buf_b):
         for k in range(3):
             buf[k, pl.ds(0, pad)] = nothing
             buf[k, pl.ds(pad + nw, pad)] = nothing
-    for ref in (xr, yr):
-        ref[pl.ds(0, 1)] = nothing[:1]
-        ref[pl.ds(nw + 1, 1)] = nothing[:1]
+    xr[pl.ds(0, 1)] = nothing[:1]
+    xr[pl.ds(nw + 1, 1)] = nothing[:1]
+
+    def pack(row, v):
+        for t in range(zt):
+            packed[pl.ds((t * ROWS + row) * ROWS, ROWS), :] = v[:, t * LANES : (t + 1) * LANES]
+
+    def to_stage(first):
+        for t in range(zt):
+            for y in range(ROWS):
+                rows = packed[pl.ds((t * ROWS + first) * ROWS + y, 4, stride=ROWS), :]
+                stage[y * zt + t, first : first + 4] = rows
+
+    for x in range(2):
+        charge = act[0][x] - act[1][x] + (1.0 - fl[x]) * fixed[x]
+        pack(4 + x, pot[x] + 2.0 * charge)
+        pack(6 + x, fl[x])
+    to_stage(4)
+
+    def over(axis, count, me, src, dst, send, recv):
+        def leaving(k):
+            peer = lax.rem(me + k, count)
+            return pltpu.make_async_remote_copy(
+                src_ref=src(peer), dst_ref=dst(me), send_sem=send.at[peer], recv_sem=recv.at[me],
+                device_id={axis: peer}, device_id_type=MESH,
+            )
+
+        def arriving(k):
+            peer = lax.rem(me + k, count)
+            return pltpu.make_async_remote_copy(
+                src_ref=src(peer), dst_ref=dst(peer), send_sem=send.at[peer], recv_sem=recv.at[peer],
+                device_id={axis: peer}, device_id_type=MESH,
+            )
+
+        def run(copy_of, act_on):
+            def body(k, _):
+                act_on(copy_of(k))
+                return 0
+
+            lax.fori_loop(1, count, body, 0)
+
+        return (
+            lambda: run(leaving, lambda c: c.start()),
+            lambda: run(arriving, lambda c: c.wait_recv()),
+            lambda: run(leaving, lambda c: c.wait_send()),
+        )
+
+    def across_wide(src, dst, send, recv):
+        return over("wide", nw, wide, src, dst, send, recv)
+
+    def across_narrow(src, dst, send, recv):
+        return over("narrow", nn, narrow, src, dst, send, recv)
+
+    early = across_wide(
+        lambda j: stage.at[j, pl.ds(4, 4)], lambda j: xr.at[j + 1, pl.ds(4, 4)], xe_s, xe_r
+    )
+    late = across_wide(
+        lambda j: stage.at[j, pl.ds(0, 4)], lambda j: xr.at[j + 1, pl.ds(0, 4)], xs_s, xs_r
+    )
+    back = across_wide(
+        lambda j: xsol.at[j, pl.ds(0, 6)], lambda j: xback.at[j, pl.ds(0, 6)], xb_s, xb_r
+    )
+    edges = across_narrow(lambda j: edge_s.at[j], lambda j: edge_r.at[j], yc_s, yc_r)
+    datum = across_narrow(lambda j: dat_s.at[j], lambda j: dat_r.at[j], ys_s, ys_r)
+    ends = across_narrow(lambda j: ends_s.at[j], lambda j: ends_r.at[j], yb_s, yb_r)
 
     pl.semaphore_wait(barrier, nw + nn - 2)
 
@@ -195,6 +260,7 @@
     ]
     for copy in halos:
         copy.start()
+    early[0]()
 
     shape = (ROWS, pot.shape[2])
     lane = lax.broadcasted_iota(jnp.int32, shape, 1)
@@ -235,17 +301,12 @@
     def kept(flag, v):
         return jnp.where(flag, v, 0.0)
 
-    def pack(row, v):
-        for t in range(zt):
-            packed[pl.ds((t * ROWS + row) * ROWS, ROWS), :] = v[:, t * LANES : (t + 1) * LANES]
-
     pots = [
         kept(has_left, rx_l[3]), kept(has_left, rx_l[4]), pot[0], pot[1],
         kept(has_right, rx_r[3]), kept(has_right, rx_r[4]),
     ]
     velx = [rx_l[2], vel[0, 0], vel[0, 1], rx_r[2]]
     for x in range(2):
-        fixed_x = fixed[x]
         p = pot[x]
         down = kept(has_down, ry_d[x])
         up = kept(has_up, ry_u[x])
@@ -265,122 +326,124 @@
             div_y = (y_next(qy, q_up) - y_prev(qy, q_down)) * 0.5
             total = div_x + div_y + div_z[x][k]
             pack(2 * k + x, fl[x] * (conc[k, x] - 0.5 * total))
-        charge = fl[x] * (conc[0, x] - conc[1, x]) + (1.0 - fl[x]) * fixed_x
-        pack(4 + x, p + 2.0 * charge)
-        pack(6 + x, fl[x])
-
-    for t in range(zt):
-        for y in range(ROWS):
-            stage[t * ROWS + y] = packed[pl.ds(t * ROWS * ROWS + y, ROWS, stride=ROWS), :]
-
-    def x_copy(k):
-        peer = lax.rem(wide + k, nw)
-        return pltpu.make_async_remote_copy(
-            src_ref=stage.at[peer], dst_ref=xr.at[wide + 1],
-            send_sem=xs_s.at[peer], recv_sem=xs_r.at[wide],
-            device_id={"wide": peer}, device_id_type=MESH,
-        )
-
-    def x_arrival(k):
-        peer = lax.rem(wide + k, nw)
-        return pltpu.make_async_remote_copy(
-            src_ref=stage.at[peer], dst_ref=xr.at[peer + 1],
-            send_sem=xs_s.at[peer], recv_sem=xs_r.at[peer],
-            device_id={"wide": peer}, device_id_type=MESH,
-        )
-
-    def back_copy(k):
-        peer = lax.rem(wide + k, nw)
-        return pltpu.make_async_remote_copy(
-            src_ref=xsol.at[peer], dst_ref=xback.at[wide],
-            send_sem=xb_s.at[peer], recv_sem=xb_r.at[wide],
-            device_id={"wide": peer}, device_id_type=MESH,
-        )
-
-    def back_arrival(k):
-        peer = lax.rem(wide + k, nw)
-        return pltpu.make_async_remote_copy(
-            src_ref=xsol.at[peer], dst_ref=xback.at[peer],
-            send_sem=xb_s.at[peer], recv_sem=xb_r.at[peer],
-            device_id={"wide": peer}, device_id_type=MESH,
-        )
-
-    def group(index):
-        return pl.ds(pl.multiple_of(index * ROWS, ROWS), ROWS)
-
-    def y_copy(k):
-        peer = lax.rem(narrow + k, nn)
-        return pltpu.make_async_remote_copy(
-            src_ref=xback.at[group(peer)], dst_ref=yr.at[pl.ds(narrow * ROWS + 1, ROWS)],
-            send_sem=ys_s.at[peer], recv_sem=ys_r.at[narrow],
-            device_id={"narrow": peer}, device_id_type=MESH,
-        )
-
-    def y_arrival(k):
-        peer = lax.rem(narrow + k, nn)
-        return pltpu.make_async_remote_copy(
-            src_ref=xback.at[group(peer)], dst_ref=yr.at[pl.ds(peer * ROWS + 1, ROWS)],
-            send_sem=ys_s.at[peer], recv_sem=ys_r.at[peer],
-            device_id={"narrow": peer}, device_id_type=MESH,
-        )
-
-    def out_copy(k):
-        peer = lax.rem(narrow + k, nn)
-        return pltpu.make_async_remote_copy(
-            src_ref=ysol.at[group(peer)], dst_ref=out.at[group(narrow)],
-            send_sem=yb_s.at[peer], recv_sem=yb_r.at[narrow],
-            device_id={"narrow": peer}, device_id_type=MESH,
-        )
-
-    def out_arrival(k):
-        peer = lax.rem(narrow + k, nn)
-        return pltpu.make_async_remote_copy(
-            src_ref=ysol.at[group(peer)], dst_ref=out.at[group(peer)],
-            send_sem=yb_s.at[peer], recv_sem=yb_r.at[peer],
-            device_id={"narrow": peer}, device_id_type=MESH,
-        )
-
-    def start(copy_of, count):
-        def body(k, _):
-            copy_of(k).start()
-            return 0
-
-        lax.fori_loop(1, count, body, 0)
-
-    def arrive(copy_of, count):
-        def body(k, _):
-            copy_of(k).wait_recv()
-            return 0
-
-        lax.fori_loop(1, count, body, 0)
-
-    def drain(copy_of, count):
-        def body(k, _):
-            copy_of(k).wait_send()
-            return 0
-
-        lax.fori_loop(1, count, body, 0)
-
-    bufs = (buf_a, buf_b)
-    start(x_copy, nw)
+    to_stage(0)
+    late[0]()
     xr[pl.ds(wide + 1, 1)] = stage[pl.ds(wide, 1)]
-    arrive(x_arrival, nw)
-    solve_tiles(xr, 1, bufs, xsol, 0, nw, pad, True)
-    start(back_copy, nw)
+
+    even, is_pot, rate = row_facts()
+
+    def y_rows(y):
+        return pl.ds(y * zt, zt)
+
+    def y_mask(y):
+        if 0 <= y < ROWS:
+            m0, m1 = masks(stage[y_rows(y)])
+        else:
+            halo, flag = (ry_d, has_down) if y < 0 else (ry_u, has_up)
+
+            def lanes(x):
+                row = kept(flag, halo[x, 5:6])
+                return jnp.stack([row[:, t * LANES : (t + 1) * LANES] for t in range(zt)])
+
+            m0, m1 = lanes(0), lanes(1)
+        return jnp.where(is_pot, 1.0, jnp.where(even, m0, m1))
+
+    before, here = y_mask(-1), y_mask(0)
+    c_prev = left_prev = None
+    for y in range(ROWS):
+        after = y_mask(y + 1)
+        rm = rate * here
+        lower = -rm * before
+        upper = -rm * after
+        if y == 0:
+            lower = kept(has_down, lower)
+        if y == ROWS - 1:
+            upper = kept(has_up, upper)
+        main = 1.0 + rm * (before + after)
+        if y == 0:
+            m = 1.0 / main
+            left_now = -lower * m
+        else:
+            m = 1.0 / (main - lower * c_prev)
+            left_now = -lower * left_prev * m
+        y_m[y_rows(y)] = m
+        y_am[y_rows(y)] = lower * m
+        c_prev, left_prev = upper * m, left_now
+        y_c[y_rows(y)] = c_prev
+        y_left[y_rows(y)] = left_now
+        before, here = here, after
+    right_now = -c_prev
+    y_right[y_rows(ROWS - 1)] = right_now
+    edge_s[:, 2] = left_prev
+    edge_s[:, 3] = right_now
+    for y in range(ROWS - 2, -1, -1):
+        c_now = y_c[y_rows(y)]
+        left_prev = y_left[y_rows(y)] - c_now * left_prev
+        right_now = -c_now * right_now
+        y_left[y_rows(y)] = left_prev
+        y_right[y_rows(y)] = right_now
+    edge_s[:, 0] = left_prev
+    edge_s[:, 1] = right_now
+    edges[0]()
+    edge_r[pl.ds(narrow, 1)] = edge_s[pl.ds(narrow, 1)]
+
+    early[1]()
+    late[1]()
+    solve_tiles(xr, 1, (buf_a, buf_b), xsol, 0, nw, pad, True)
+    back[0]()
     xback[pl.ds(wide, 1)] = xsol[pl.ds(wide, 1)]
-    arrive(back_arrival, nw)
-    start(y_copy, nn)
-    yr[pl.ds(narrow * ROWS + 1, ROWS)] = xback[group(narrow)]
-    arrive(y_arrival, nn)
-    solve_tiles(yr, 1, bufs, ysol, 0, nn * ROWS, pad, False)
-    start(out_copy, nn)
-    out[group(narrow)] = ysol[group(narrow)]
-    arrive(out_arrival, nn)
-    drain(x_copy, nw)
-    drain(back_copy, nw)
-    drain(y_copy, nn)
-    drain(out_copy, nn)
-
+
+    edges[1]()
+    gain = jnp.zeros((ROWS, LANES), F32)
+    for n in range(nn):
+        first_left, first_right, last_left, last_right = (edge_r[n, i] for i in range(4))
+        q = 1.0 / (1.0 - first_left * gain)
+        ring[n, 0] = q
+        ring[n, 1] = q * first_left
+        ring[n, 2] = last_left * gain
+        ring[n, 3] = q * first_right
+        gain = last_right + last_left * gain * (q * first_right)
+        ring[n, 4] = gain
+
+    back[1]()
+    d = xback[y_rows(0)] * y_m[y_rows(0)]
+    y_sol[y_rows(0)] = d
+    for y in range(1, ROWS):
+        d = xback[y_rows(y)] * y_m[y_rows(y)] - y_am[y_rows(y)] * d
+        y_sol[y_rows(y)] = d
+    dat_s[:, 1] = d
+    for y in range(ROWS - 2, -1, -1):
+        d = y_sol[y_rows(y)] - y_c[y_rows(y)] * d
+        y_sol[y_rows(y)] = d
+    dat_s[:, 0] = d
+    datum[0]()
+    dat_r[pl.ds(narrow, 1)] = dat_s[pl.ds(narrow, 1)]
+    datum[1]()
+    firsts, lasts = [], []
+    last = jnp.zeros((ROWS, LANES), F32)
+    for n in range(nn):
+        first = ring[n, 0] * dat_r[n, 0] + ring[n, 1] * last
+        last = dat_r[n, 1] + edge_r[n, 2] * last + ring[n, 2] * first
+        firsts.append(first)
+        lasts.append(last)
+    following = jnp.zeros((ROWS, LANES), F32)
+    for n in range(nn - 1, -1, -1):
+        ends_s[n, 1] = following
+        following = firsts[n] + ring[n, 3] * following
+        if n > 0:
+            ends_s[n, 0] = lasts[n - 1] + ring[n - 1, 4] * following
+        else:
+            ends_s[n, 0] = jnp.zeros((ROWS, LANES), F32)
+    ends[0]()
+    ends_r[pl.ds(narrow, 1)] = ends_s[pl.ds(narrow, 1)]
+    ends[1]()
+    from_left, from_right = ends_r[:, 0], ends_r[:, 1]
+    for y in range(ROWS):
+        out[y_rows(y)] = (
+            y_sol[y_rows(y)] + y_left[y_rows(y)] * from_left + y_right[y_rows(y)] * from_right
+        )
+    for exchange in (early, late, back, edges, datum, ends):
+        exchange[2]()
 
 def z_kernel(tiles, solid, new_conc, new_pot):
     length = solid.shape[2]
@@ -392,7 +455,7 @@
     def source(row):
         return jnp.concatenate(
             [
-                tiles[pl.ds(t * ROWS * ROWS + row, ROWS, stride=ROWS), :]
+                tiles[pl.ds(t * ROWS + row, ROWS, stride=length // LANES * ROWS), :]
                 for t in range(length // LANES)
             ],
             axis=1,
@@ -458,9 +521,12 @@
             scratch_shapes=[pltpu.VMEM(plane, F32)] * 4
             + [pltpu.VMEM(edge, F32)] * 4
             + [pltpu.VMEM((nw * ROWS, LANES), F32)]
-            + [pltpu.VMEM(s, F32) for s in (tiles, padded, tiles, tiles, padded, tiles, bands, bands)]
-            + [dma((4,)), dma((4,)), dma((nw,)), dma((nw,)), dma((nw,)), dma((nw,))]
-            + [dma((nn,)), dma((nn,)), dma((nn,)), dma((nn,))],
+            + [pltpu.VMEM(s, F32) for s in (tiles, padded, tiles, tiles, bands, bands)]
+            + [pltpu.VMEM(tiles, F32)] * 6
+            + [pltpu.VMEM((nn, n, ROWS, LANES), F32) for n in (4, 4, 2, 2, 2, 2, 5)]
+            + [dma((4,))] * 2
+            + [dma((nw,))] * 6
+            + [dma((nn,))] * 6,
             compiler_params=pltpu.CompilerParams(collective_id=0, has_side_effects=True),
         )(conc, potential, velocity, solid, fixed_charge)
         return pl.pallas_call(

time: 73.3 us -> 66.2 us (0.903)
  Pallas kernels: 72.5 us -> 65.4 us
    pallas_call x1, Pallas kernels: 67.8 us -> 60.7 us  [shards(): pl.pallas_call(body, name='halo_x_y', out_shape=jax.ShapeDtypeStruct(tile...]
where the time goes in v2:
time: 66.2 us; the launch traced here: 66.1 us
  Pallas kernels  65.4 us (99%)
    pallas_call x1, Pallas kernels, shards(): pl.pallas_call(body, name='halo_x_y', out_shape=jax.ShapeDtypeStruct(tile...  60.7 us
    pallas_call x1, Pallas kernels, shards(): pl.pallas_call(z_kernel, name='solve_z', out_shape=(jax.ShapeDtypeStruct(...  4.75 us

profile of v2, /device:TPU:1, one launch (start us, length us, event | category | flops | bytes accessed | tf_op | source)
XLA Modules:
  0.0 66.1 jit_solution(11340607626087807023)
XLA Ops:
  0.6 60.7 %halo_x_y.1 = f32[64,8,128]{2,1,0:T(8,128)} custom-call(f32[2,2,8,1024]{3,2,1,0:T(8,128)} %refs_0_.1, f32[2,8,1024]{2,1,0:T(8,128)} %refs_1_.1, f32[3,2,8,1024]{3,2,1,0:T(8,128)} %refs_2_.1, s32[2,8,1024]{2,1,0:T(8,128)} %solid.1, f32[2,8,1024]{2,1,0:T(8,128)} %refs_4_.1), custom_call_target="tpu_custom_call" | custom-call | tf_op jit(solution)/shard_map/halo_x_y/pallas_call | solution.py:515
  61.3 4.7 %solve_z.1 = (f32[2,2,8,1024]{3,2,1,0:T(8,128)}, f32[2,8,1024]{2,1,0:T(8,128)}) custom-call(f32[512,128]{1,0:T(8,128)} %bitcast.1, s32[2,8,1024]{2,1,0:T(8,128)} %solid.1), custom_call_target="tpu_custom_call" | custom-call | tf_op jit(solution)/shard_map/solve_z/pallas_call | solution.py:532

commit v3 on v2

--- a/solution.py
+++ b/solution.py
@@ -117,12 +117,60 @@
         spacing *= 2
 
 
+def z_reduce(solid, z_inv, z_steps, length):
+    shape = (ROWS, length)
+    lane = lax.broadcasted_iota(jnp.int32, shape, 1)
+    for case in range(5):
+        if case < 4:
+            rm = (8.0, 5.0)[case // 2] * (1 - solid[case % 2]).astype(F32)
+            mask = (1 - solid[case % 2]).astype(F32)
+            before = jnp.where(lane == 0, 0.0, pltpu.roll(mask, 1, 1))
+            after = jnp.where(lane == length - 1, 0.0, pltpu.roll(mask, length - 1, 1))
+            inv = 1.0 / (1.0 + rm * (before + after))
+            lower, upper = -rm * before * inv, -rm * after * inv
+        else:
+            inv = jnp.full(shape, 1.0 / 33.0, F32)
+            lower = jnp.where(lane == 0, 0.0, -16.0 * inv)
+            upper = jnp.where(lane == length - 1, 0.0, -16.0 * inv)
+        z_inv[case] = inv
+        spacing, step = 1, 0
+        while spacing < length:
+            lower_prev, upper_prev = (pltpu.roll(v, spacing, 1) for v in (lower, upper))
+            lower_next, upper_next = (pltpu.roll(v, length - spacing, 1) for v in (lower, upper))
+            r = 1.0 / (1.0 - lower * upper_prev - upper * lower_next)
+            lower, upper = lower * r, upper * r
+            for k, v in enumerate((r, lower, upper)):
+                z_steps[case, step, k] = v
+            lower, upper = -lower * lower_prev, -upper * upper_next
+            spacing, step = spacing * 2, step + 1
+
+
+def z_solve(packed, field, z_inv, z_steps, length):
+    cases = [min(2 * field + x, 4) for x in range(2)]
+    values = []
+    for x in range(2):
+        parts = [
+            packed[pl.ds((t * ROWS + 2 * field + x) * ROWS, ROWS), :] for t in range(length // LANES)
+        ]
+        values.append(jnp.concatenate(parts, axis=1) * z_inv[cases[x]])
+    spacing, step = 1, 0
+    while spacing < length:
+        for x in range(2):
+            d = values[x]
+            r, lower, upper = (z_steps[cases[x], step, k] for k in range(3))
+            values[x] = (
+                d * r - lower * pltpu.roll(d, spacing, 1) - upper * pltpu.roll(d, length - spacing, 1)
+            )
+        spacing, step = spacing * 2, step + 1
+    return values
+
+
 def main_kernel(
-    nw, nn, conc, pot, vel, solid, fixed, out,
+    nw, nn, conc, pot, vel, solid, fixed, new_conc, new_pot,
     sx_r, sx_l, rx_l, rx_r, sy_u, sy_d, ry_d, ry_u, packed, stage, xr, xsol, xback,
     buf_a, buf_b, y_am, y_m, y_c, y_left, y_right, y_sol,
-    edge_s, edge_r, dat_s, dat_r, ends_s, ends_r, ring,
-    hs, hr, xe_s, xe_r, xs_s, xs_r, xb_s, xb_r, yc_s, yc_r, ys_s, ys_r, yb_s, yb_r,
+    edge_s, edge_r, dat_s, dat_r, ends_s, ends_r, ring, z_inv, z_steps,
+    hs, hr, xs_s, xs_r, xb_s, xb_r, yc_s, yc_r, ys_s, ys_r, yb_s, yb_r,
 ):
     wide = lax.axis_index("wide")
     narrow = lax.axis_index("narrow")
@@ -229,12 +277,7 @@
     def across_narrow(src, dst, send, recv):
         return over("narrow", nn, narrow, src, dst, send, recv)
 
-    early = across_wide(
-        lambda j: stage.at[j, pl.ds(4, 4)], lambda j: xr.at[j + 1, pl.ds(4, 4)], xe_s, xe_r
-    )
-    late = across_wide(
-        lambda j: stage.at[j, pl.ds(0, 4)], lambda j: xr.at[j + 1, pl.ds(0, 4)], xs_s, xs_r
-    )
+    lines = across_wide(lambda j: stage.at[j], lambda j: xr.at[j + 1], xs_s, xs_r)
     back = across_wide(
         lambda j: xsol.at[j, pl.ds(0, 6)], lambda j: xback.at[j, pl.ds(0, 6)], xb_s, xb_r
     )
@@ -260,7 +303,6 @@
     ]
     for copy in halos:
         copy.start()
-    early[0]()
 
     shape = (ROWS, pot.shape[2])
     lane = lax.broadcasted_iota(jnp.int32, shape, 1)
@@ -327,7 +369,7 @@
             total = div_x + div_y + div_z[x][k]
             pack(2 * k + x, fl[x] * (conc[k, x] - 0.5 * total))
     to_stage(0)
-    late[0]()
+    lines[0]()
     xr[pl.ds(wide + 1, 1)] = stage[pl.ds(wide, 1)]
 
     even, is_pot, rate = row_facts()
@@ -387,11 +429,11 @@
     edges[0]()
     edge_r[pl.ds(narrow, 1)] = edge_s[pl.ds(narrow, 1)]
 
-    early[1]()
-    late[1]()
+    lines[1]()
     solve_tiles(xr, 1, (buf_a, buf_b), xsol, 0, nw, pad, True)
     back[0]()
     xback[pl.ds(wide, 1)] = xsol[pl.ds(wide, 1)]
+    z_reduce(solid, z_inv, z_steps, length)
 
     edges[1]()
     gain = jnp.zeros((ROWS, LANES), F32)
@@ -439,62 +481,17 @@
     ends[1]()
     from_left, from_right = ends_r[:, 0], ends_r[:, 1]
     for y in range(ROWS):
-        out[y_rows(y)] = (
-            y_sol[y_rows(y)] + y_left[y_rows(y)] * from_left + y_right[y_rows(y)] * from_right
-        )
-    for exchange in (early, late, back, edges, datum, ends):
+        value = y_sol[y_rows(y)] + y_left[y_rows(y)] * from_left + y_right[y_rows(y)] * from_right
+        for t in range(zt):
+            packed[pl.ds(t * ROWS * ROWS + y, ROWS, stride=ROWS), :] = value[t]
+    for k in range(3):
+        for x, value in enumerate(z_solve(packed, k, z_inv, z_steps, length)):
+            if k < 2:
+                new_conc[k, x] = value
+            else:
+                new_pot[x] = value
+    for exchange in (lines, back, edges, datum, ends):
         exchange[2]()
-
-def z_kernel(tiles, solid, new_conc, new_pot):
-    length = solid.shape[2]
-    shape = (ROWS, length)
-    lane = lax.broadcasted_iota(jnp.int32, shape, 1)
-    first = lane == 0
-    last = lane == length - 1
-
-    def source(row):
-        return jnp.concatenate(
-            [
-                tiles[pl.ds(t * ROWS + row, ROWS, stride=length // LANES * ROWS), :]
-                for t in range(length // LANES)
-            ],
-            axis=1,
-        )
-
-    def solve(lower, upper, sources):
-        spacing = 1
-        while spacing < length:
-            lower_prev, upper_prev = (pltpu.roll(v, spacing, 1) for v in (lower, upper))
-            lower_next, upper_next = (pltpu.roll(v, length - spacing, 1) for v in (lower, upper))
-            r = 1.0 / (1.0 - lower * upper_prev - upper * lower_next)
-            sources = [
-                (d - lower * pltpu.roll(d, spacing, 1) - upper * pltpu.roll(d, length - spacing, 1)) * r
-                for d in sources
-            ]
-            lower, upper = -(lower * lower_prev) * r, -(upper * upper_next) * r
-            spacing *= 2
-        return sources
-
-    for x in range(2):
-        mask = (1 - solid[x]).astype(F32)
-        before = jnp.where(first, 0.0, pltpu.roll(mask, 1, 1))
-        after = jnp.where(last, 0.0, pltpu.roll(mask, length - 1, 1))
-        for k, rate in enumerate((8.0, 5.0)):
-            rm = rate * mask
-            inv = 1.0 / (1.0 + rm * (before + after))
-            (result,) = solve(
-                -rm * before * inv, -rm * after * inv, [source(2 * k + x) * inv]
-            )
-            new_conc[k, x] = result
-    inv = 1.0 / 33.0
-    results = solve(
-        jnp.where(first, 0.0, -16.0 * inv) * jnp.ones(shape, F32),
-        jnp.where(last, 0.0, -16.0 * inv) * jnp.ones(shape, F32),
-        [source(4) / 33.0, source(5) / 33.0],
-    )
-    for x in range(2):
-        new_pot[x] = results[x]
-
 
 def solution(mesh):
     nw, nn = mesh.shape["wide"], mesh.shape["narrow"]
@@ -512,33 +509,28 @@
         def body(*refs):
             main_kernel(nw, nn, *refs)
 
-        after_y = pl.pallas_call(
+        return pl.pallas_call(
             body,
-            name="halo_x_y",
-            out_shape=jax.ShapeDtypeStruct(tiles, F32),
+            name="adi_step",
+            out_shape=(
+                jax.ShapeDtypeStruct(conc.shape, F32),
+                jax.ShapeDtypeStruct(potential.shape, F32),
+            ),
             in_specs=[vmem] * 5,
-            out_specs=vmem,
+            out_specs=(vmem, vmem),
             scratch_shapes=[pltpu.VMEM(plane, F32)] * 4
             + [pltpu.VMEM(edge, F32)] * 4
             + [pltpu.VMEM((nw * ROWS, LANES), F32)]
             + [pltpu.VMEM(s, F32) for s in (tiles, padded, tiles, tiles, bands, bands)]
             + [pltpu.VMEM(tiles, F32)] * 6
             + [pltpu.VMEM((nn, n, ROWS, LANES), F32) for n in (4, 4, 2, 2, 2, 2, 5)]
+            + [pltpu.VMEM((5, ROWS, height), F32)]
+            + [pltpu.VMEM((5, (height - 1).bit_length(), 3, ROWS, height), F32)]
             + [dma((4,))] * 2
-            + [dma((nw,))] * 6
+            + [dma((nw,))] * 4
             + [dma((nn,))] * 6,
             compiler_params=pltpu.CompilerParams(collective_id=0, has_side_effects=True),
         )(conc, potential, velocity, solid, fixed_charge)
-        return pl.pallas_call(
-            z_kernel,
-            name="solve_z",
-            out_shape=(
-                jax.ShapeDtypeStruct(conc.shape, F32),
-                jax.ShapeDtypeStruct(potential.shape, F32),
-            ),
-            in_specs=[vmem] * 2,
-            out_specs=(vmem, vmem),
-        )(after_y.reshape(nw * ROWS, LANES), solid)
 
     return jax.shard_map(
         shards,

time: 66.2 us -> 65.3 us (0.986)
  Pallas kernels: 65.4 us -> 62.3 us
  local copies, waits for them, and re-layouts: 0 us -> 2.23 us
    pallas_call x2 -> x1, Pallas kernels: 65.4 us -> 62.3 us  [shards(): pl.pallas_call(body, name='adi_step', out_shape=(jax.ShapeDtypeStruct(con...]
    unnamed x0 -> x4, local copies, waits for them, and re-layouts: none -> 2.23 us
where the time goes in v3:
time: 65.3 us; the launch traced here: 65.2 us
  Pallas kernels  62.3 us (95%)
  local copies, waits for them, and re-layouts  2.23 us (3%)
    pallas_call x1, Pallas kernels, shards(): pl.pallas_call(body, name='adi_step', out_shape=(jax.ShapeDtypeStruct(con...  62.3 us
    unnamed x4, local copies, waits for them, and re-layouts  2.23 us

profile of v3, /device:TPU:1, one launch (start us, length us, event | category | flops | bytes accessed | tf_op | source)
XLA Modules:
  0.0 65.2 jit_solution(18204219831350638455)
XLA Ops:
  0.6 62.3 %adi_step.1 = (f32[2,2,8,1024]{3,2,1,0:T(8,128)}, f32[2,8,1024]{2,1,0:T(8,128)}) custom-call(f32[2,2,8,1024]{3,2,1,0:T(8,128)} %refs_0_.1, f32[2,8,1024]{2,1,0:T(8,128)} %refs_1_.1, f32[3,2,8,1024]{3,2,1,0:T(8,128)} %refs_2_.1, s32[2,8,1024]{2,1,0:T(8,128)} %refs_3_.1, f32[2,8,1024]{2,1,0:T(8,128)} %refs_4_.1), custom_call_target="tpu_custom_call" | custom-call | tf_op jit(solution)/shard_map/adi_step/pallas_call | solution.py:512
  62.9 0.0 copy-start
  62.9 1.6 %copy.9 = f32[2,2,8,1024]{3,2,1,0:T(8,128)} copy(f32[2,2,8,1024]{3,2,1,0:T(8,128)} %get-tuple-element.4) | data formatting | bytes 262144
  64.5 0.0 copy-done
  64.5 0.6 copy.10
Async XLA Ops:
  62.9 1.6 %copy-start = (f32[2,8,1024]{2,1,0:T(8,128)S(1)}, f32[2,8,1024]{2,1,0:T(8,128)}, u32[]{:S(2)}) copy-start(f32[2,8,1024]{2,1,0:T(8,128)} %get-tuple-element.5) | copy-start | bytes 196612

commit v4 on v3

--- a/solution.py
+++ b/solution.py
@@ -166,7 +166,8 @@
 
 
 def main_kernel(
-    nw, nn, conc, pot, vel, solid, fixed, new_conc, new_pot,
+    nw, nn, conc_in, pot_in, vel_in, solid_in, fixed_in, new_conc, new_pot,
+    conc, pot, vel, solid, fixed, in_sem,
     sx_r, sx_l, rx_l, rx_r, sy_u, sy_d, ry_d, ry_u, packed, stage, xr, xsol, xback,
     buf_a, buf_b, y_am, y_m, y_c, y_left, y_right, y_sol,
     edge_s, edge_r, dat_s, dat_r, ends_s, ends_r, ring, z_inv, z_steps,
@@ -181,6 +182,16 @@
     zt = pot.shape[2] // LANES
     pad = (buf_a.shape[1] - nw) // 2
 
+    loads = [
+        pltpu.make_async_copy(src, dst, in_sem.at[n])
+        for n, (src, dst) in enumerate(
+            (
+                (solid_in, solid), (conc_in, conc), (pot_in, pot), (vel_in, vel), (fixed_in, fixed)
+            )
+        )
+    ]
+    for load in loads:
+        load.start()
     barrier = pltpu.get_barrier_semaphore()
 
     def greet_wide(k, _):
@@ -198,6 +209,8 @@
     lax.fori_loop(1, nw, greet_wide, 0)
     lax.fori_loop(1, nn, greet_narrow, 0)
 
+    for load in loads:
+        load.wait()
     fl = [(1 - solid[x]).astype(F32) for x in range(2)]
     act = [[fl[x] * conc[k, x] for x in range(2)] for k in range(2)]
     for k in range(2):
@@ -282,8 +295,12 @@
         lambda j: xsol.at[j, pl.ds(0, 6)], lambda j: xback.at[j, pl.ds(0, 6)], xb_s, xb_r
     )
     edges = across_narrow(lambda j: edge_s.at[j], lambda j: edge_r.at[j], yc_s, yc_r)
-    datum = across_narrow(lambda j: dat_s.at[j], lambda j: dat_r.at[j], ys_s, ys_r)
-    ends = across_narrow(lambda j: ends_s.at[j], lambda j: ends_r.at[j], yb_s, yb_r)
+    datum = across_narrow(
+        lambda j: dat_s.at[j, :, pl.ds(0, 6)], lambda j: dat_r.at[j, :, pl.ds(0, 6)], ys_s, ys_r
+    )
+    ends = across_narrow(
+        lambda j: ends_s.at[j, :, pl.ds(0, 6)], lambda j: ends_r.at[j, :, pl.ds(0, 6)], yb_s, yb_r
+    )
 
     pl.semaphore_wait(barrier, nw + nn - 2)
 
@@ -332,6 +349,7 @@
             row.append((z_next(q) - z_prev(q)) * 0.5)
         div_z.append(row)
 
+    z_reduce(solid, z_inv, z_steps, length)
     for copy in halos:
         copy.wait()
 
@@ -433,7 +451,6 @@
     solve_tiles(xr, 1, (buf_a, buf_b), xsol, 0, nw, pad, True)
     back[0]()
     xback[pl.ds(wide, 1)] = xsol[pl.ds(wide, 1)]
-    z_reduce(solid, z_inv, z_steps, length)
 
     edges[1]()
     gain = jnp.zeros((ROWS, LANES), F32)
@@ -493,6 +510,11 @@
     for exchange in (lines, back, edges, datum, ends):
         exchange[2]()
 
+def hand_on(conc, pot, new_conc, new_pot):
+    new_conc[...] = conc[...]
+    new_pot[...] = pot[...]
+
+
 def solution(mesh):
     nw, nn = mesh.shape["wide"], mesh.shape["narrow"]
 
@@ -509,16 +531,24 @@
         def body(*refs):
             main_kernel(nw, nn, *refs)
 
-        return pl.pallas_call(
+        results = pl.pallas_call(
             body,
             name="adi_step",
             out_shape=(
                 jax.ShapeDtypeStruct(conc.shape, F32),
                 jax.ShapeDtypeStruct(potential.shape, F32),
             ),
-            in_specs=[vmem] * 5,
+            in_specs=[pl.BlockSpec(memory_space=pl.ANY)] * 5,
             out_specs=(vmem, vmem),
-            scratch_shapes=[pltpu.VMEM(plane, F32)] * 4
+            scratch_shapes=[
+                pltpu.VMEM(conc.shape, F32),
+                pltpu.VMEM(potential.shape, F32),
+                pltpu.VMEM(velocity.shape, F32),
+                pltpu.VMEM(solid.shape, jnp.int32),
+                pltpu.VMEM(fixed_charge.shape, F32),
+                dma((5,)),
+            ]
+            + [pltpu.VMEM(plane, F32)] * 4
             + [pltpu.VMEM(edge, F32)] * 4
             + [pltpu.VMEM((nw * ROWS, LANES), F32)]
             + [pltpu.VMEM(s, F32) for s in (tiles, padded, tiles, tiles, bands, bands)]
@@ -531,6 +561,13 @@
             + [dma((nn,))] * 6,
             compiler_params=pltpu.CompilerParams(collective_id=0, has_side_effects=True),
         )(conc, potential, velocity, solid, fixed_charge)
+        return pl.pallas_call(
+            hand_on,
+            name="hand_on",
+            out_shape=tuple(jax.ShapeDtypeStruct(r.shape, F32) for r in results),
+            in_specs=[vmem, vmem],
+            out_specs=(vmem, vmem),
+        )(*results)
 
     return jax.shard_map(
         shards,

time: 65.3 us -> 63.4 us (0.971)
  local copies, waits for them, and re-layouts: 2.23 us -> 0 us
    unnamed x4 -> x0, local copies, waits for them, and re-layouts: 2.23 us -> none
    pallas_call x0 -> x1, Pallas kernels: none -> 1.59 us  [shards(): pl.pallas_call(hand_on, name='hand_on', out_shape=tuple((jax.ShapeDtypeSt...]
    pallas_call x1, Pallas kernels: 62.3 us -> 61 us  [shards(): pl.pallas_call(body, name='adi_step', out_shape=(jax.ShapeDtypeStruct(con...]
where the time goes in v4:
time: 63.4 us; the launch traced here: 63.2 us
  Pallas kernels  62.6 us (99%)
  between operations  0.64 us (1%)
    pallas_call x1, Pallas kernels, shards(): pl.pallas_call(body, name='adi_step', out_shape=(jax.ShapeDtypeStruct(con...  61 us
    pallas_call x1, Pallas kernels, shards(): pl.pallas_call(hand_on, name='hand_on', out_shape=tuple((jax.ShapeDtypeSt...  1.59 us

profile of v4, /device:TPU:1, one launch (start us, length us, event | category | flops | bytes accessed | tf_op | source)
XLA Modules:
  0.0 63.2 jit_solution(11717871367549017879)
XLA Ops:
  0.6 61.0 %adi_step.1 = (f32[2,2,8,1024]{3,2,1,0:T(8,128)}, f32[2,8,1024]{2,1,0:T(8,128)}) custom-call(f32[2,2,8,1024]{3,2,1,0:T(8,128)} %refs_0_.1, f32[2,8,1024]{2,1,0:T(8,128)} %refs_1_.1, f32[3,2,8,1024]{3,2,1,0:T(8,128)} %refs_2_.1, s32[2,8,1024]{2,1,0:T(8,128)} %refs_3_.1, f32[2,8,1024]{2,1,0:T(8,128)} %refs_4_.1), custom_call_target="tpu_custom_call" | custom-call | tf_op jit(solution)/shard_map/adi_step/pallas_call | solution.py:534
  61.6 1.6 %hand_on.1 = (f32[2,2,8,1024]{3,2,1,0:T(8,128)}, f32[2,8,1024]{2,1,0:T(8,128)}) custom-call(f32[2,2,8,1024]{3,2,1,0:T(8,128)} %get-tuple-element.4.conc, f32[2,8,1024]{2,1,0:T(8,128)} %get-tuple-element.5.pot), custom_call_target="tpu_custom_call" | custom-call | tf_op jit(solution)/shard_map/hand_on/pallas_call | solution.py:564

commit v5 on v4

--- a/solution.py
+++ b/solution.py
@@ -196,7 +196,7 @@
 
     def greet_wide(k, _):
         pl.semaphore_signal(
-            barrier, inc=1, device_id={"wide": lax.rem(wide + k, nw)}, device_id_type=MESH
+            barrier, inc=1, device_id={"wide": lax.rem(wide + nw // 2 + k, nw)}, device_id_type=MESH
         )
         return 0
 
@@ -206,7 +206,8 @@
         )
         return 0
 
-    lax.fori_loop(1, nw, greet_wide, 0)
+    lax.fori_loop(0, nw // 2, greet_wide, 0)
+    lax.fori_loop(nw // 2 + 1, nw, greet_wide, 0)
     lax.fori_loop(1, nn, greet_narrow, 0)
 
     for load in loads:
@@ -534,11 +535,8 @@
         results = pl.pallas_call(
             body,
             name="adi_step",
-            out_shape=(
-                jax.ShapeDtypeStruct(conc.shape, F32),
-                jax.ShapeDtypeStruct(potential.shape, F32),
-            ),
-            in_specs=[pl.BlockSpec(memory_space=pl.ANY)] * 5,
+            out_shape=(pltpu.VMEM(conc.shape, F32), pltpu.VMEM(potential.shape, F32)),
+            in_specs=[pl.BlockSpec(memory_space=pltpu.HBM)] * 5,
             out_specs=(vmem, vmem),
             scratch_shapes=[
                 pltpu.VMEM(conc.shape, F32),
@@ -559,11 +557,14 @@
             + [dma((4,))] * 2
             + [dma((nw,))] * 4
             + [dma((nn,))] * 6,
-            compiler_params=pltpu.CompilerParams(collective_id=0, has_side_effects=True),
+            compiler_params=pltpu.CompilerParams(
+                collective_id=0, has_side_effects=True, vmem_limit_bytes=65000 * 1024
+            ),
         )(conc, potential, velocity, solid, fixed_charge)
         return pl.pallas_call(
             hand_on,
             name="hand_on",
+            compiler_params=pltpu.CompilerParams(vmem_limit_bytes=16 * 2**20),
             out_shape=tuple(jax.ShapeDtypeStruct(r.shape, F32) for r in results),
             in_specs=[vmem, vmem],
             out_specs=(vmem, vmem),

time: 63.4 us -> 61.6 us (0.972)
  Pallas kernels: 62.6 us -> 60.9 us
    pallas_call x2, Pallas kernels: 62.6 us -> 60.9 us  [the longest x1 60.2 us: shards(): pl.pallas_call(body, name='adi_step', out_shape=(pltpu.VMEM(conc.shape, F...]
where the time goes in v5:
time: 61.6 us; the launch traced here: 61.5 us
  Pallas kernels  60.9 us (99%)
  between operations  0.64 us (1%)
    pallas_call x1, Pallas kernels, shards(): pl.pallas_call(body, name='adi_step', out_shape=(pltpu.VMEM(conc.shape, F...  60.2 us

profile of v5, /device:TPU:1, one launch (start us, length us, event | category | flops | bytes accessed | tf_op | source)
XLA Modules:
  0.0 61.5 jit_solution(3027022885514978320)
XLA Ops:
  0.6 60.2 %adi_step.1 = (f32[2,2,8,1024]{3,2,1,0:T(8,128)S(1)}, f32[2,8,1024]{2,1,0:T(8,128)S(1)}) custom-call(f32[2,2,8,1024]{3,2,1,0:T(8,128)} %refs_0_.1, f32[2,8,1024]{2,1,0:T(8,128)} %refs_1_.1, f32[3,2,8,1024]{3,2,1,0:T(8,128)} %refs_2_.1, s32[2,8,1024]{2,1,0:T(8,128)} %refs_3_.1, f32[2,8,1024]{2,1,0:T(8,128)} %refs_4_.1), custom_call_target="tpu_custom_call" | custom-call | tf_op jit(solution)/shard_map/adi_step/pallas_call | solution.py:535
  60.8 0.7 %hand_on.1 = (f32[2,2,8,1024]{3,2,1,0:T(8,128)}, f32[2,8,1024]{2,1,0:T(8,128)}) custom-call(f32[2,2,8,1024]{3,2,1,0:T(8,128)S(1)} %get-tuple-element.4.conc, f32[2,8,1024]{2,1,0:T(8,128)S(1)} %get-tuple-element.5.pot), custom_call_target="tpu_custom_call" | custom-call | tf_op jit(solution)/shard_map/hand_on/pallas_call | solution.py:564

commit v6 on v5

--- a/solution.py
+++ b/solution.py
@@ -233,30 +233,6 @@
         sy_d[x, 5:6] = fl[x][0:1]
         sy_u[x, 6:8] = jnp.zeros((2, pot.shape[2]), F32)
         sy_d[x, 6:8] = jnp.zeros((2, pot.shape[2]), F32)
-    nothing = jnp.zeros((pad, ROWS, LANES), F32)
-    for buf in (buf_a, buf_b):
-        for k in range(3):
-            buf[k, pl.ds(0, pad)] = nothing
-            buf[k, pl.ds(pad + nw, pad)] = nothing
-    xr[pl.ds(0, 1)] = nothing[:1]
-    xr[pl.ds(nw + 1, 1)] = nothing[:1]
-
-    def pack(row, v):
-        for t in range(zt):
-            packed[pl.ds((t * ROWS + row) * ROWS, ROWS), :] = v[:, t * LANES : (t + 1) * LANES]
-
-    def to_stage(first):
-        for t in range(zt):
-            for y in range(ROWS):
-                rows = packed[pl.ds((t * ROWS + first) * ROWS + y, 4, stride=ROWS), :]
-                stage[y * zt + t, first : first + 4] = rows
-
-    for x in range(2):
-        charge = act[0][x] - act[1][x] + (1.0 - fl[x]) * fixed[x]
-        pack(4 + x, pot[x] + 2.0 * charge)
-        pack(6 + x, fl[x])
-    to_stage(4)
-
     def over(axis, count, me, src, dst, send, recv):
         def leaving(k):
             peer = lax.rem(me + k, count)
@@ -321,6 +297,31 @@
     ]
     for copy in halos:
         copy.start()
+
+    nothing = jnp.zeros((pad, ROWS, LANES), F32)
+    for buf in (buf_a, buf_b):
+        for k in range(3):
+            buf[k, pl.ds(0, pad)] = nothing
+            buf[k, pl.ds(pad + nw, pad)] = nothing
+    xr[pl.ds(0, 1)] = nothing[:1]
+    xr[pl.ds(nw + 1, 1)] = nothing[:1]
+
+    def pack(row, v):
+        for t in range(zt):
+            packed[pl.ds((t * ROWS + row) * ROWS, ROWS), :] = v[:, t * LANES : (t + 1) * LANES]
+
+    def to_stage(first):
+        for t in range(zt):
+            for y in range(ROWS):
+                rows = packed[pl.ds((t * ROWS + first) * ROWS + y, 4, stride=ROWS), :]
+                stage[y * zt + t, first : first + 4] = rows
+
+    for x in range(2):
+        charge = act[0][x] - act[1][x] + (1.0 - fl[x]) * fixed[x]
+        pack(4 + x, pot[x] + 2.0 * charge)
+        pack(6 + x, fl[x])
+    to_stage(4)
+
 
     shape = (ROWS, pot.shape[2])
     lane = lax.broadcasted_iota(jnp.int32, shape, 1)

time: 61.6 us -> 61.6 us (level)
  no operation moved by 1% of the time
where the time goes in v6:
time: 61.6 us; the launch traced here: 61.5 us
  Pallas kernels  60.9 us (99%)
  between operations  0.64 us (1%)
    pallas_call x1, Pallas kernels, shards(): pl.pallas_call(body, name='adi_step', out_shape=(pltpu.VMEM(conc.shape, F...  60.2 us

profile of v6, /device:TPU:1, one launch (start us, length us, event | category | flops | bytes accessed | tf_op | source)
XLA Modules:
  0.0 61.5 jit_solution(8985152916642028625)
XLA Ops:
  0.6 60.2 %adi_step.1 = (f32[2,2,8,1024]{3,2,1,0:T(8,128)S(1)}, f32[2,8,1024]{2,1,0:T(8,128)S(1)}) custom-call(f32[2,2,8,1024]{3,2,1,0:T(8,128)} %refs_0_.1, f32[2,8,1024]{2,1,0:T(8,128)} %refs_1_.1, f32[3,2,8,1024]{3,2,1,0:T(8,128)} %refs_2_.1, s32[2,8,1024]{2,1,0:T(8,128)} %refs_3_.1, f32[2,8,1024]{2,1,0:T(8,128)} %refs_4_.1), custom_call_target="tpu_custom_call" | custom-call | tf_op jit(solution)/shard_map/adi_step/pallas_call | solution.py:536
  60.8 0.7 %hand_on.1 = (f32[2,2,8,1024]{3,2,1,0:T(8,128)}, f32[2,8,1024]{2,1,0:T(8,128)}) custom-call(f32[2,2,8,1024]{3,2,1,0:T(8,128)S(1)} %get-tuple-element.4.conc, f32[2,8,1024]{2,1,0:T(8,128)S(1)} %get-tuple-element.5.pot), custom_call_target="tpu_custom_call" | custom-call | tf_op jit(solution)/shard_map/hand_on/pallas_call | solution.py:565
